TPU v7x, 512 devices: a whole 4x8x8 slice. The times are simulated.
512 devices in a mesh: ctx: 16 (over z_hi, x), exp: 32 (over z_lo, y, core).
Axes of the slice: x: 4, y: 8, z: 8 (z_hi: 4, z_lo: 2; z = z_hi * 2 + z_lo), core: 2. Of those that a mesh axis runs over, the one named last changes fastest.
Arguments:
- hidden: bfloat16 [32, 128, 5120], P('exp', 'ctx'), may hold values from -6 to 6
- queries: bfloat16 [2048, 36864], P('ctx', 'exp'), may hold values from -50 to 50
- latents: bfloat16 [2048, 576], P('ctx'), may hold values from -6.5 to 6.5
- expert_ids: int32 [32, 128, 6], P('exp', 'ctx'), may hold values from 0 to 31, all different within a row; in each aligned block of 8 rows (0 to 7, 8 to 15, ..., all dimensions but the last counted through in order) at most 2 rows name the same one
- route_weight: float32 [32, 128, 6], P('exp', 'ctx'), may hold values from 0.1 to 1
- w_gate: bfloat16 [32, 1536, 5120], P('exp', 'ctx'), may hold values from -0.078125 to 0.078125
- w_up: bfloat16 [32, 1536, 5120], P('exp', 'ctx'), may hold values from -0.078125 to 0.078125
- w_down: bfloat16 [32, 5120, 1536], P('exp', 'ctx'), may hold values from -0.15625 to 0.15625
Outputs:
- attended: bfloat16 [2048, 32768], P('ctx', 'exp')
- moe_out: bfloat16 [32, 128, 5120], P('exp', 'ctx')
Inputs may be any that keep to these rules, and one draw needn't show every extreme that they name: `expert_ids`: each token names 6 different experts. Within the 8 rows of one device (aligned blocks of rows of one group) no expert is named by more than 2 rows, a bound that some block reaches.
All inputs are finite; a program needn't handle non-finite values.
Results may differ from a plain program's by a relative error of at most 0.0057.
Values may be sent and summed in bfloat16 or wider, within the bound.
A program may use at most 64 MiB of HBM per device.

v0:
```python
import jax
import jax.numpy as jnp
from jax import lax
from jax.sharding import PartitionSpec as P

LATENT = 512
ROPE = 64


SCALE = 0.07216878364870322


def shifted(block, axis, distance):
    devices = range(lax.axis_size(axis))
    route = [(i - distance, i) for i in devices if i - distance in devices]
    return lax.ppermute(block, axis, route)


def place_picks(picks, experts, capacity):
    flat = picks.reshape(-1)
    onehot = (flat[:, None] == jnp.arange(experts, dtype=jnp.int32)[None, :]).astype(jnp.int32)
    earlier = jnp.cumsum(onehot, axis=0) - onehot
    rank = jnp.sum(earlier * onehot, axis=1)
    target = flat * capacity + rank
    return (target[:, None] == jnp.arange(experts * capacity, dtype=jnp.int32)[None, :]).astype(
        jnp.float32
    )


def token_table(tok_count, topk):
    owner = jnp.arange(tok_count * topk, dtype=jnp.int32) // topk
    return (owner[:, None] == jnp.arange(tok_count, dtype=jnp.int32)[None, :]).astype(jnp.float32)


def times_rows(left, right):
    return lax.dot_general(
        left, right, (((1,), (1,)), ((), ())), preferred_element_type=jnp.float32
    )


def on_device(hidden, queries, latents, expert_ids, route_weight, w_gate, w_up, w_down):
    tok_att = latents.shape[0]
    heads_dev = queries.shape[1] // (LATENT + ROPE)
    tok_dev = hidden.shape[1]
    width = hidden.shape[2]
    topk = expert_ids.shape[2]
    experts = lax.axis_size("exp")
    groups = lax.axis_size("ctx")
    capacity = min(tok_dev, max(2, 3 * topk * tok_dev // (2 * experts)))
    slots = experts * capacity
    earlier_kv = shifted(latents, "ctx", 1)
    keys = jnp.concatenate([earlier_kv, latents], axis=0)
    query_rows = queries.reshape(tok_att, heads_dev, LATENT + ROPE)
    scores = jnp.einsum("thc,kc->htk", query_rows, keys, preferred_element_type=jnp.float32) * SCALE
    row_pos = jnp.arange(tok_att, dtype=jnp.int32)
    key_pos = jnp.arange(2 * tok_att, dtype=jnp.int32)
    seen_own = (key_pos[None, :] >= tok_att) & (key_pos[None, :] - tok_att <= row_pos[:, None])
    seen_prev = (key_pos[None, :] < tok_att) & (lax.axis_index("ctx") > 0)
    scores = jnp.where((seen_own | seen_prev)[None, :, :], scores, jnp.float32(-1e30))
    top = jnp.max(scores, axis=-1, keepdims=True)
    expo = jnp.exp(scores - top)
    probs = (expo / jnp.sum(expo, axis=-1, keepdims=True)).astype(jnp.bfloat16)
    mixed_heads = jnp.einsum(
        "htk,kc->thc", probs, keys[:, :LATENT], preferred_element_type=jnp.float32
    )
    attended = mixed_heads.astype(jnp.bfloat16).reshape(tok_att, heads_dev * LATENT)
    tokens = hidden[0]
    picks = expert_ids[0]
    pick_weight = route_weight[0].reshape(-1)
    tok_hot = token_table(tok_dev, topk)
    slot_hot = place_picks(picks, experts, capacity)
    gate_w = w_gate[0]
    up_w = w_up[0]
    down_w = w_down[0]
    send_matrix = jnp.dot(slot_hot.T, tok_hot).astype(jnp.bfloat16)
    outgoing = jnp.dot(send_matrix, tokens, preferred_element_type=jnp.float32).astype(jnp.bfloat16)
    outgoing = outgoing.reshape(experts, capacity, width)
    arrived = lax.all_to_all(outgoing, "exp", split_axis=0, concat_axis=0, tiled=True)
    piece = lax.all_gather(arrived.reshape(slots, width), "ctx", axis=0, tiled=True)
    gate = times_rows(piece, gate_w)
    upper = times_rows(piece, up_w)
    hidden_units = (jax.nn.silu(gate) * upper).astype(jnp.bfloat16)
    projected = times_rows(lax.all_gather(hidden_units, "ctx", axis=1, tiled=True), down_w)
    columns = projected.astype(jnp.bfloat16).reshape(groups, experts, capacity, down_w.shape[0])
    by_block = lax.all_to_all(columns, "ctx", split_axis=0, concat_axis=3, tiled=True)
    returned = lax.all_to_all(by_block, "exp", split_axis=1, concat_axis=1, tiled=True)
    combine_matrix = jnp.dot(
        slot_hot.T, tok_hot * pick_weight[:, None], precision=lax.Precision.HIGHEST
    )
    back_rows = returned.reshape(slots, width).astype(jnp.float32)
    mixed = jnp.dot(combine_matrix.T, back_rows, precision=lax.Precision.HIGHEST).astype(
        jnp.bfloat16
    )
    return (attended, mixed[None])


def solution(mesh):
    placed = (
        P("exp", "ctx", None),
        P("ctx", "exp"),
        P("ctx", None),
        P("exp", "ctx", None),
        P("exp", "ctx", None),
        P("exp", "ctx", None),
        P("exp", "ctx", None),
        P("exp", "ctx", None),
    )
    return jax.shard_map(
        on_device,
        mesh=mesh,
        in_specs=placed,
        out_specs=(P("ctx", "exp"), P("exp", "ctx", None)),
        check_vma=False,
    )
```

profile of v0, /device:TPU:1, one launch (start us, length us, event | category | flops | bytes accessed | tf_op | source)
XLA Modules:
  0.0 342.5 jit_solution(18093524210329897696)
XLA Ops:
  7.2 0.9 copy.32
  8.1 0.1 reshape_squeeze.3
  8.4 0.2 select_reduce_fusion
  8.6 1.5 convolution_convert_fusion
  10.1 0.2 reshape.116
  10.3 29.4 %all_to_all.28 = bf16[32,2,5120]{2,1,0:T(2,128)(2,1)S(1)} all-to-all(bf16[32,2,5120]{2,1,0:T(2,128)(2,1)S(1)} %reshape.116), channel_id=1, replica_groups=mesh['ctx'=16,'exp'=32] {'exp'}, dimensions={0} | all-to-all | bytes 1310720 | tf_op jit(solution)/shard_map/all_to_all | solution.py:78
  39.7 1.1 reshape.117
  40.9 126.4 %all-gather.3.cloned.1.call-done = bf16[1024,5120]{1,0:T(8,128)(2,1)} async-done(((bf16[64,5120]{1,0:T(8,128)(2,1)}), bf16[1024,5120]{1,0:T(8,128)(2,1)}) %all-gather.3.cloned.1.call-update) | async-done | bytes 10485776 | tf_op jit(solution)/shard_map/all_gather | solution.py:79
  167.3 7.7 %fusion.9 = f32[1024,96]{0,1:T(8,128)S(1)} fusion(bf16[1024,5120]{1,0:T(8,128)(2,1)} %all-gather.3.cloned.1.call-done, bf16[1,96,5120]{2,1,0:T(8,128)(2,1)} %param.13), kind=kOutput, calls=%fused_computation.16 | convolution fusion | flops 1006632960 | bytes 11862016 | tf_op jit(solution)/shard_map/dot_general | solution.py:36
  175.1 4.1 %fusion.3 = bf16[1024,96]{0,1:T(8,128)(2,1)} fusion(bf16[1024,5120]{1,0:T(8,128)(2,1)S(1)} %copy-done.1, bf16[1,96,5120]{2,1,0:T(8,128)(2,1)S(1)} %copy-done.5, f32[1024,96]{0,1:T(8,128)S(1)} %fusion.9), kind=kOutput, calls=%fused_computation.8 | convolution fusion | flops 1007222784 | bytes 12058624 | tf_op jit(solution)/shard_map/dot_general | solution.py:36
  179.2 91.1 %all-gather.5.cloned.1.call-done = bf16[1024,1536]{0,1:T(8,128)(2,1)} async-done(((bf16[1024,96]{0,1:T(8,128)(2,1)}), bf16[1024,1536]{0,1:T(8,128)(2,1)}) %all-gather.5.cloned.1.call-update) | async-done | bytes 3145744 | tf_op jit(solution)/shard_map/all_gather | solution.py:83
  270.2 3.1 convolution_convert_fusion.2
  273.3 0.4 copy.34
  273.7 1.2 reshape.118
  274.9 6.0 %all-to-all-start.1 = ((bf16[16,32,2,320]{3,2,1,0:T(2,128)(2,1)}), bf16[16,32,2,320]{3,2,1,0:T(2,128)(2,1)S(1)}, u32[]{:S(2)}, u32[]{:S(2)}) async-start(bf16[16,32,2,320]{3,2,1,0:T(2,128)(2,1)} %reshape.118), calls=%async_computation.1 | async-start | bytes 1572864 | tf_op jit(solution)/shard_map/all_to_all | solution.py:85
  281.0 3.3 collective-permute-start
  284.3 0.1 copy.33
  284.3 0.1 mul.45
  284.4 0.2 copy.30
  284.7 18.0 %all-to-all-done.1 = bf16[16,32,2,320]{3,2,1,0:T(2,128)(2,1)S(1)} async-done(((bf16[16,32,2,320]{3,2,1,0:T(2,128)(2,1)}), bf16[16,32,2,320]{3,2,1,0:T(2,128)(2,1)S(1)}, u32[]{:S(2)}, u32[]{:S(2)}) %all-to-all-start.1) | async-done | bytes 655392 | tf_op jit(solution)/shard_map/all_to_all | solution.py:85
  302.7 0.7 copy.39
  303.4 1.7 reshape.122
  305.1 10.3 %all-to-all-start.2 = ((bf16[1,32,2,5120]{3,2,0,1:T(2,128)(2,1)}), bf16[1,32,2,5120]{3,2,0,1:T(2,128)(2,1)S(1)}, u32[]{:S(2)}, u32[]{:S(2)}) async-start(bf16[1,32,2,5120]{3,2,0,1:T(2,128)(2,1)} %reshape.122), calls=%async_computation.2 | async-start | bytes 1310720 | tf_op jit(solution)/shard_map/all_to_all | solution.py:86
  315.4 0.2 fusion.14
  315.6 0.3 fusion.16
  315.9 0.3 fusion.5
  316.2 0.1 fusion.29
  316.4 0.3 convolution_convert_fusion.3
  316.6 0.9 copy.37
  317.5 16.9 %all-to-all-done.2 = bf16[1,32,2,5120]{3,2,0,1:T(2,128)(2,1)S(1)} async-done(((bf16[1,32,2,5120]{3,2,0,1:T(2,128)(2,1)}), bf16[1,32,2,5120]{3,2,0,1:T(2,128)(2,1)S(1)}, u32[]{:S(2)}, u32[]{:S(2)}) %all-to-all-start.2) | async-done | bytes 655392 | tf_op jit(solution)/shard_map/all_to_all | solution.py:86
  334.4 0.2 reshape.119
  334.7 1.0 fusion.1
  (24 shorter events, 0.4 us)
Async XLA Ops:
  7.2 263.1 %copy-start = (bf16[1,320,1536]{2,1,0:T(8,128)(2,1)S(1)}, bf16[1,320,1536]{2,1,0:T(8,128)(2,1)}, u32[]{:S(2)}) copy-start(bf16[1,320,1536]{2,1,0:T(8,128)(2,1)} %param.15) | copy-start | bytes 2949124
  7.2 167.8 %copy-start.5 = (bf16[1,96,5120]{2,1,0:T(8,128)(2,1)S(1)}, bf16[1,96,5120]{2,1,0:T(8,128)(2,1)}, u32[]{:S(2)}) copy-start(bf16[1,96,5120]{2,1,0:T(8,128)(2,1)} %param.14) | copy-start | bytes 2949124
  7.2 160.1 %all-gather.3.cloned.1.call-start = ((), (), s32[]{:S(2)}) async-start(), calls=%async_computation.3 | async-start | bytes 11141120 | tf_op jit(solution)/shard_map/all_gather | solution.py:79
  40.8 229.4 %all-gather.5.cloned.1.call-start = ((), (), s32[]{:S(2)}) async-start(), calls=%async_computation.4 | async-start | bytes 3342336 | tf_op jit(solution)/shard_map/all_gather | solution.py:83
  167.3 7.7 %copy-start.1 = (bf16[1024,5120]{1,0:T(8,128)(2,1)S(1)}, bf16[1024,5120]{1,0:T(8,128)(2,1)}, u32[]{:S(2)}) copy-start(bf16[1024,5120]{1,0:T(8,128)(2,1)} %all-gather.3.cloned.1.call-done) | copy-start | bytes 31457284
  175.0 105.9 %copy-start.3 = (bf16[128,576]{0,1:T(8,128)(2,1)S(1)}, bf16[128,576]{0,1:T(8,128)(2,1)}, u32[]{:S(2)}) copy-start(bf16[128,576]{0,1:T(8,128)(2,1)} %param.10) | copy-start | bytes 442372
  175.0 109.2 %copy-start.4 = (f32[1,8,6]{1,0,2:T(1,128)S(1)}, f32[1,8,6]{1,0,2:T(1,128)}, u32[]{:S(2)}) copy-start(f32[1,8,6]{1,0,2:T(1,128)} %param.12) | copy-start | bytes 580
  175.0 109.4 %copy-start.2 = (bf16[128,1152]{1,0:T(8,128)(2,1)S(1)}, bf16[128,1152]{1,0:T(8,128)(2,1)}, u32[]{:S(2)}) copy-start(bf16[128,1152]{1,0:T(8,128)(2,1)} %param.9) | copy-start | bytes 884740
  274.9 27.8 %all-to-all-start.1 = ((bf16[16,32,2,320]{3,2,1,0:T(2,128)(2,1)}), bf16[16,32,2,320]{3,2,1,0:T(2,128)(2,1)S(1)}, u32[]{:S(2)}, u32[]{:S(2)}) async-start(bf16[16,32,2,320]{3,2,1,0:T(2,128)(2,1)} %reshape.118), calls=%async_computation.1 | async-start | bytes 1572864 | tf_op jit(solution)/shard_map/all_to_all | solution.py:85
  281.0 34.9 %collective-permute-start = (bf16[128,576]{0,1:T(8,128)(2,1)S(1)}, bf16[128,576]{0,1:T(8,128)(2,1)S(1)}, u32[]{:S(2)}, u32[]{:S(2)}) collective-permute-start(bf16[128,576]{0,1:T(8,128)(2,1)S(1)} %copy-done.3), channel_id=1, source_target_pairs={{0,32},{32,64},{64,96},{96,128},{128,160},{160,192},{192,224},{224... | collective-permute-start | bytes 442376 | tf_op jit(solution)/shard_map/ppermute | solution.py:16
  305.1 29.3 %all-to-all-start.2 = ((bf16[1,32,2,5120]{3,2,0,1:T(2,128)(2,1)}), bf16[1,32,2,5120]{3,2,0,1:T(2,128)(2,1)S(1)}, u32[]{:S(2)}, u32[]{:S(2)}) async-start(bf16[1,32,2,5120]{3,2,0,1:T(2,128)(2,1)} %reshape.122), calls=%async_computation.2 | async-start | bytes 1310720 | tf_op jit(solution)/shard_map/all_to_all | solution.py:86
Sparse Core Ops, SparseCore 0:
  40.9 126.3 all-gather.2
  179.3 90.9 all-gather.4
where the time goes:
time: 343 us; the launch traced here: 342 us
  waiting for transfers between devices  252 us (73%)
  blocking collectives  29.4 us (9%)
  starting transfers between devices  19.7 us (6%)
  matrix products  18.2 us (5%)
  between operations  14.2 us (4%)
  local copies, waits for them, and re-layouts  7.93 us (2%)
    all_gather x1, waiting for transfers between devices, on_device(): lax.all_gather(arrived.reshape(slots, width), 'ctx', axis=0, tiled=True)  126 us
    all_gather x1, waiting for transfers between devices, on_device(): lax.all_gather(hidden_units, 'ctx', axis=1, tiled=True)  91.1 us
    all_to_all x1, blocking collectives, on_device(): lax.all_to_all(outgoing, 'exp', split_axis=0, concat_axis=0, tiled=True)  29.4 us
    all_to_all x1, waiting for transfers between devices, on_device(): lax.all_to_all(columns, 'ctx', split_axis=0, concat_axis=3, tiled=True)  18 us
    all_to_all x1, waiting for transfers between devices, on_device(): lax.all_to_all(by_block, 'exp', split_axis=1, concat_axis=1, tiled=True)  16.9 us
    dot_general x3, matrix products, times_rows(): lax.dot_general(left, right, (((1,), (1,)), ((), ())), preferred_element_...  14.8 us
    all_to_all x1, starting transfers between devices, on_device(): lax.all_to_all(by_block, 'exp', split_axis=1, concat_axis=1, tiled=True)  10.3 us
  transfers between devices with their start and end apart: 5, of which 4 were waited for; matrix products, arithmetic and copies ran while one was open for 1% of the time, Pallas kernels for 0%

commit v1 on v0

v1 whole, which is shorter than its diff:
```python
import functools

import jax
import jax.numpy as jnp
from jax import lax
from jax.experimental import pallas as pl
from jax.experimental.pallas import tpu as pltpu
from jax.sharding import PartitionSpec as P

LATENT = 512
ROPE = 64
SCALE = 0.07216878364870322
NX = 4
NZ = 4
CAP = 2
MESH = pl.DeviceIdType.MESH
F32, BF16 = jnp.float32, jnp.bfloat16


def shifted(block, axis, distance):
    devices = range(lax.axis_size(axis))
    route = [(i - distance, i) for i in devices if i - distance in devices]
    return lax.ppermute(block, axis, route)


def dot_nt(left, right):
    return lax.dot_general(left, right, (((1,), (1,)), ((), ())), preferred_element_type=F32)


def flat(ref):
    blocks, inner, width = ref.shape
    return ref[...].reshape(blocks * inner, width)


def moe_kernel(
    n_exp,
    tok_ref, pick_ref, weight_ref, wg_ref, wu_ref, wd_ref, out_ref,
    tokens, table, own_table, packed, rows, gate_w, up_w, down_w, act, y_send, y_recv, mixed, final,
    local_sem, tok_s, tok_r, table_s, table_r, row_s, row_r, w_s, w_r, act_s, act_r, y_s, y_r, fin_s, fin_r,
):
    c, e = lax.axis_index("ctx"), lax.axis_index("exp")
    z, x = c // NX, c % NX
    tok, width = tok_ref.shape[1], tok_ref.shape[2]
    units, cols = wg_ref.shape[1], wd_ref.shape[1]
    chunk = NZ * CAP
    slots = n_exp * chunk
    out_cols = NX * cols
    right = (z * NX + (x + 1) % NX, e)
    left = (z * NX + (x + NX - 1) % NX, e)
    x_left, x_right = (x + NX - 1) % NX, (x + 1) % NX

    def z_peer(d):
        return ((z + d) % NZ) * NX + x

    def at(ref, index, size):
        return ref.at[pl.ds(pl.multiple_of(index * size, size), size), :]

    own = [
        pltpu.make_async_copy(src.at[0], at(dst, x, size), local_sem.at[i])
        for i, (src, dst, size) in enumerate(
            ((wg_ref, gate_w, units), (wu_ref, up_w, units), (wd_ref, down_w, cols))
        )
    ]
    for copy in own:
        copy.start()

    barrier = pltpu.get_barrier_semaphore()

    def greet(d, carry):
        pl.semaphore_signal(barrier, inc=1, device_id=(c, lax.rem(e + d, n_exp)), device_id_type=MESH)
        return carry

    lax.fori_loop(1, n_exp, greet, 0)
    for d in range(1, NZ):
        pl.semaphore_signal(barrier, inc=1, device_id=(z_peer(d), e), device_id_type=MESH)
    for peer in (left, right):
        pl.semaphore_signal(barrier, inc=1, device_id=peer, device_id_type=MESH)

    lane = lax.broadcasted_iota(jnp.int32, (tok, slots), 1)
    lane_expert, lane_z, lane_rank = lane // chunk, (lane % chunk) // CAP, lane % CAP
    picks, weights = pick_ref[0], weight_ref[0]
    named = jnp.zeros((tok, slots), F32)
    coef = jnp.zeros((tok, slots), F32)
    for k in range(picks.shape[1]):
        hit = picks[:, k : k + 1] == lane_expert
        named = jnp.where(hit, 1.0, named)
        coef = jnp.where(hit, weights[:, k : k + 1], coef)
    before = lax.broadcasted_iota(jnp.int32, (tok, tok), 1) < lax.broadcasted_iota(jnp.int32, (tok, tok), 0)
    rank = jnp.dot(jnp.where(before, 1.0, 0.0), named, preferred_element_type=F32)
    here = (lane_z == z) & (rank == lane_rank.astype(F32))
    own_table[0:tok, :] = jnp.where(here, coef, 0.0)
    own_table[tok : 2 * tok, :] = jnp.where(here, named, 0.0)

    pl.semaphore_wait(barrier, n_exp - 1 + NZ - 1 + 2)

    def remote(src, dst, send, recv, peer):
        return pltpu.make_async_remote_copy(
            src_ref=src, dst_ref=dst, send_sem=send, recv_sem=recv, device_id=peer, device_id_type=MESH
        )

    for d in range(1, NZ):
        remote(own_table, table.at[z], table_s.at[d], table_r.at[z], (z_peer(d), e)).start()
        remote(tok_ref.at[0], tokens.at[z], tok_s.at[d], tok_r.at[z], (z_peer(d), e)).start()
    tokens[z] = tok_ref[0]
    table[z] = own_table[...]

    own[0].wait()
    own[1].wait()
    mine_g, mine_u = at(gate_w, x, units), at(up_w, x, units)
    to_right = [
        remote(mine_g, mine_g, w_s.at[0], w_r.at[0], right),
        remote(mine_u, mine_u, w_s.at[1], w_r.at[1], right),
    ]
    to_left = [
        remote(mine_u, mine_u, w_s.at[2], w_r.at[2], left),
        remote(mine_g, mine_g, w_s.at[3], w_r.at[3], left),
    ]
    for a, b in zip(to_right, to_left):
        a.start()
        b.start()

    for d in range(1, NZ):
        p = (z + d) % NZ
        remote(own_table, table.at[p], table_s.at[d], table_r.at[p], (c, e)).wait_recv()
        remote(tok_ref.at[0], tokens.at[p], tok_s.at[d], tok_r.at[p], (c, e)).wait_recv()

    select = jnp.concatenate([table[i, tok : 2 * tok, :] for i in range(NZ)], axis=0)
    select = jnp.transpose(select, (1, 0)).astype(BF16)
    picked = jnp.dot(select, flat(tokens), preferred_element_type=F32)
    packed[...] = picked.reshape(packed.shape).astype(BF16)

    def row_copy(peer, src_index, dst_index, s, r):
        return remote(packed.at[src_index], rows.at[dst_index], row_s.at[s], row_r.at[r], (c, peer))

    def send_rows(d, carry):
        peer = lax.rem(e + d, n_exp)
        row_copy(peer, peer, e, peer, e).start()
        return carry

    lax.fori_loop(1, n_exp, send_rows, 0)
    rows[e] = packed[e]

    theirs_g, theirs_u = at(gate_w, x_left, units), at(up_w, x_right, units)
    remote(theirs_g, theirs_g, w_s.at[0], w_r.at[0], right).wait_recv()
    on_right = remote(theirs_g, theirs_g, w_s.at[4], w_r.at[4], right)
    on_right.start()
    remote(theirs_u, theirs_u, w_s.at[2], w_r.at[2], left).wait_recv()
    on_left = remote(theirs_u, theirs_u, w_s.at[5], w_r.at[5], left)
    on_left.start()
    to_right[0].wait_send()
    to_right[1].wait_send()
    to_left[0].wait_send()
    to_left[1].wait_send()
    up_left, gate_right = at(up_w, x_left, units), at(gate_w, x_right, units)
    remote(up_left, up_left, w_s.at[1], w_r.at[1], right).wait_recv()
    remote(gate_right, gate_right, w_s.at[3], w_r.at[3], left).wait_recv()
    on_right.wait_send()
    on_left.wait_send()
    far = (x + 2) % NX
    far_g, far_u = at(gate_w, far, units), at(up_w, far, units)

    own[2].wait()
    mine_d = at(down_w, x, cols)
    d_right = remote(mine_d, mine_d, w_s.at[6], w_r.at[6], right)
    d_left = remote(mine_d, mine_d, w_s.at[7], w_r.at[7], left)
    d_right.start()
    d_left.start()

    remote(far_g, far_g, w_s.at[4], w_r.at[4], right).wait_recv()
    remote(far_u, far_u, w_s.at[5], w_r.at[5], left).wait_recv()

    def take_rows(d, carry):
        peer = lax.rem(e + d, n_exp)
        row_copy(e, peer, peer, peer, peer).wait_recv()
        return carry

    lax.fori_loop(1, n_exp, take_rows, 0)

    chosen = flat(rows)
    gate = dot_nt(chosen, gate_w[...])
    upper = dot_nt(chosen, up_w[...])
    act[z] = (gate / (1.0 + jnp.exp(-gate)) * upper).astype(BF16)
    for d in range(1, NZ):
        remote(act.at[z], act.at[z], act_s.at[d], act_r.at[z], (z_peer(d), e)).start()

    half = cols // 2

    def half_of(index, part):
        return down_w.at[pl.ds(pl.multiple_of(index * cols + part * half, half), half), :]

    left_d, right_d = at(down_w, x_left, cols), at(down_w, x_right, cols)
    remote(left_d, left_d, w_s.at[6], w_r.at[6], right).wait_recv()
    f_right = remote(half_of(x_left, 0), half_of(x_left, 0), w_s.at[8], w_r.at[8], right)
    f_right.start()
    remote(right_d, right_d, w_s.at[7], w_r.at[7], left).wait_recv()
    f_left = remote(half_of(x_right, 1), half_of(x_right, 1), w_s.at[9], w_r.at[9], left)
    f_left.start()
    for d in range(1, NZ):
        p = (z + d) % NZ
        remote(act.at[p], act.at[p], act_s.at[d], act_r.at[p], (c, e)).wait_recv()
    remote(half_of(far, 0), half_of(far, 0), w_s.at[8], w_r.at[8], right).wait_recv()
    remote(half_of(far, 1), half_of(far, 1), w_s.at[9], w_r.at[9], left).wait_recv()

    y = jnp.zeros((slots, out_cols), F32)
    per_z = NX * units
    for i in range(NZ):
        y = y + dot_nt(act[i], down_w[:, i * per_z : (i + 1) * per_z])
    y_send[...] = y.reshape(y_send.shape).astype(BF16)

    def y_copy(peer, src_index, dst_index, s, r):
        return remote(y_send.at[src_index], y_recv.at[dst_index], y_s.at[s], y_r.at[r], (c, peer))

    def send_y(d, carry):
        peer = lax.rem(e + d, n_exp)
        y_copy(peer, peer, e, peer, e).start()
        return carry

    lax.fori_loop(1, n_exp, send_y, 0)
    y_recv[e] = y_send[e]

    def take_y(d, carry):
        peer = lax.rem(e + d, n_exp)
        y_copy(e, peer, peer, peer, peer).wait_recv()
        return carry

    lax.fori_loop(1, n_exp, take_y, 0)

    combine = jnp.concatenate([table[i, 0:tok, :] for i in range(NZ)], axis=0)
    high = combine.astype(BF16)
    low = (combine - high.astype(F32)).astype(BF16)
    arrived = flat(y_recv)
    total = jnp.dot(high, arrived, preferred_element_type=F32)
    total = total + jnp.dot(low, arrived, preferred_element_type=F32)
    mixed[...] = total.reshape(mixed.shape).astype(BF16)

    def columns(index):
        return final.at[:, pl.ds(pl.multiple_of(index * out_cols, out_cols), out_cols)]

    for d in range(1, NZ):
        p = (z + d) % NZ
        remote(mixed.at[p], columns(z), fin_s.at[d], fin_r.at[z], (z_peer(d), e)).start()
    columns(z)[...] = mixed[z]
    for d in range(1, NZ):
        p = (z + d) % NZ
        remote(mixed.at[p], columns(p), fin_s.at[d], fin_r.at[p], (c, e)).wait_recv()
    out_ref[0] = final[...]

    for d in range(1, NZ):
        p = (z + d) % NZ
        remote(own_table, table.at[z], table_s.at[d], table_r.at[z], (z_peer(d), e)).wait_send()
        remote(tok_ref.at[0], tokens.at[z], tok_s.at[d], tok_r.at[z], (z_peer(d), e)).wait_send()
        remote(act.at[z], act.at[z], act_s.at[d], act_r.at[z], (z_peer(d), e)).wait_send()
        remote(mixed.at[p], columns(z), fin_s.at[d], fin_r.at[z], (z_peer(d), e)).wait_send()
    for copy in (d_right, d_left, f_right, f_left):
        copy.wait_send()

    def sent(d, carry):
        peer = lax.rem(e + d, n_exp)
        row_copy(peer, peer, e, peer, e).wait_send()
        y_copy(peer, peer, e, peer, e).wait_send()
        return carry

    lax.fori_loop(1, n_exp, sent, 0)


def routed(hidden, expert_ids, route_weight, w_gate, w_up, w_down):
    n_exp = lax.axis_size("exp")
    tok, width = hidden.shape[1:]
    units, hid = w_gate.shape[1], w_down.shape[2]
    cols = w_down.shape[1]
    slots = n_exp * NZ * CAP
    dma = pltpu.SemaphoreType.DMA
    vmem = pl.BlockSpec(memory_space=pltpu.VMEM)
    hbm = pl.BlockSpec(memory_space=pl.ANY)
    return pl.pallas_call(
        functools.partial(moe_kernel, n_exp),
        out_shape=jax.ShapeDtypeStruct(hidden.shape, BF16),
        in_specs=[vmem, vmem, vmem, hbm, hbm, hbm],
        out_specs=vmem,
        scratch_shapes=[
            pltpu.VMEM((NZ, tok, width), BF16),
            pltpu.VMEM((NZ, 2 * tok, slots), F32),
            pltpu.VMEM((2 * tok, slots), F32),
            pltpu.VMEM((n_exp, NZ * CAP, width), BF16),
            pltpu.VMEM((n_exp, NZ * CAP, width), BF16),
            pltpu.VMEM((NX * units, width), BF16),
            pltpu.VMEM((NX * units, width), BF16),
            pltpu.VMEM((NX * cols, hid), BF16),
            pltpu.VMEM((NZ, slots, NX * units), BF16),
            pltpu.VMEM((n_exp, NZ * CAP, NX * cols), BF16),
            pltpu.VMEM((n_exp, NZ * CAP, NX * cols), BF16),
            pltpu.VMEM((NZ, tok, NX * cols), BF16),
            pltpu.VMEM((tok, width), BF16),
            dma((3,)),
            dma((NZ,)), dma((NZ,)), dma((NZ,)), dma((NZ,)),
            dma((n_exp,)), dma((n_exp,)),
            dma((10,)), dma((10,)),
            dma((NZ,)), dma((NZ,)),
            dma((n_exp,)), dma((n_exp,)),
            dma((NZ,)), dma((NZ,)),
        ],
        compiler_params=pltpu.CompilerParams(
            collective_id=0, has_side_effects=True, vmem_limit_bytes=50 << 20
        ),
    )(hidden, expert_ids, route_weight, w_gate, w_up, w_down)


def on_device(hidden, queries, latents, expert_ids, route_weight, w_gate, w_up, w_down):
    tok_att = latents.shape[0]
    heads_dev = queries.shape[1] // (LATENT + ROPE)
    earlier_kv = shifted(latents, "ctx", 1)
    keys = jnp.concatenate([earlier_kv, latents], axis=0)
    query_rows = queries.reshape(tok_att, heads_dev, LATENT + ROPE)
    scores = jnp.einsum("thc,kc->htk", query_rows, keys, preferred_element_type=F32) * SCALE
    row_pos = jnp.arange(tok_att, dtype=jnp.int32)
    key_pos = jnp.arange(2 * tok_att, dtype=jnp.int32)
    seen_own = (key_pos[None, :] >= tok_att) & (key_pos[None, :] - tok_att <= row_pos[:, None])
    seen_prev = (key_pos[None, :] < tok_att) & (lax.axis_index("ctx") > 0)
    scores = jnp.where((seen_own | seen_prev)[None, :, :], scores, jnp.float32(-1e30))
    top = jnp.max(scores, axis=-1, keepdims=True)
    expo = jnp.exp(scores - top)
    probs = (expo / jnp.sum(expo, axis=-1, keepdims=True)).astype(BF16)
    mixed_heads = jnp.einsum("htk,kc->thc", probs, keys[:, :LATENT], preferred_element_type=F32)
    attended = mixed_heads.astype(BF16).reshape(tok_att, heads_dev * LATENT)
    moe_out = routed(hidden, expert_ids, route_weight, w_gate, w_up, w_down)
    return attended, moe_out


def solution(mesh):
    placed = (
        P("exp", "ctx", None),
        P("ctx", "exp"),
        P("ctx", None),
        P("exp", "ctx", None),
        P("exp", "ctx", None),
        P("exp", "ctx", None),
        P("exp", "ctx", None),
        P("exp", "ctx", None),
    )
    return jax.shard_map(
        on_device,
        mesh=mesh,
        in_specs=placed,
        out_specs=(P("ctx", "exp"), P("exp", "ctx", None)),
        check_vma=False,
    )
```

time: 343 us -> 151 us (0.44)
  waiting for transfers between devices: 252 us -> 0.01 us
  Pallas kernels: 0 us -> 138 us
  blocking collectives: 29.4 us -> 0 us
  matrix products: 18.2 us -> 0.58 us
  starting transfers between devices: 19.7 us -> 3.96 us
  between operations: 14.2 us -> 0.75 us
    all_gather x2 -> x0, waiting for transfers between devices: 218 us -> none  [the longest x1 126 us: on_device(): lax.all_gather(arrived.reshape(slots, width), 'ctx', axis=0, tiled=True)]
    pallas_call x0 -> x1, Pallas kernels: none -> 138 us  [routed(): pl.pallas_call(functools.partial(moe_kernel, n_exp), out_shape=jax.ShapeD...]
    all_to_all x2 -> x0, waiting for transfers between devices: 34.9 us -> none  [the longest x1 18 us: on_device(): lax.all_to_all(columns, 'ctx', split_axis=0, concat_axis=3, tiled=True)]
    all_to_all x1 -> x0, blocking collectives: 29.4 us -> none  [on_device(): lax.all_to_all(outgoing, 'exp', split_axis=0, concat_axis=0, tiled=True)]
    dot_general x7 -> x1, matrix products: 17.9 us -> 0.3 us  [on_device(): jnp.einsum('thc,kc->htk', query_rows, keys, preferred_element_type=F32)]
    all_to_all x2 -> x0, starting transfers between devices: 16.3 us -> none  [the longest x1 10.3 us: on_device(): lax.all_to_all(by_block, 'exp', split_axis=1, concat_axis=1, tiled=True)]
    unnamed x17 -> x20, local copies, waits for them, and re-layouts: 2.12 us -> 7.95 us
  transfers between devices with their start and end apart: 5 -> 1, of which waited for: 4 -> 0; matrix products, arithmetic and copies ran while one was open for 1% -> 1% of each run, Pallas kernels for 0% -> 91%
where the time goes in v1:
time: 151 us
  Pallas kernels  138 us (91%)
  local copies, waits for them, and re-layouts  7.99 us (5%)
  starting transfers between devices  3.96 us (3%)
    pallas_call x1, Pallas kernels, routed(): pl.pallas_call(functools.partial(moe_kernel, n_exp), out_shape=jax.ShapeD...  138 us
    unnamed x20, local copies, waits for them, and re-layouts  7.95 us
    ppermute x1, starting transfers between devices, shifted(): return lax.ppermute(block, axis, route)  3.96 us
  transfers between devices with their start and end apart: 1, of which 0 were waited for; matrix products, arithmetic and copies ran while one was open for 1% of the time, Pallas kernels for 91%

profile of v1, /device:TPU:1, one launch (start us, length us, event | category | flops | bytes accessed | tf_op | source)
XLA Modules:
  0.0 151.2 jit_solution(13735026988142152429)
XLA Ops:
  0.6 4.0 %collective-permute-start = (bf16[128,576]{0,1:T(8,128)(2,1)}, bf16[128,576]{0,1:T(8,128)(2,1)S(1)}, u32[]{:S(2)}, u32[]{:S(2)}) collective-permute-start(bf16[128,576]{0,1:T(8,128)(2,1)} %param.10), channel_id=1, source_target_pairs={{0,32},{32,64},{64,96},{96,128},{128,160},{160,192},{192,224},{224... | collective-permute-start | bytes 442376 | tf_op jit(solution)/shard_map/ppermute | solution.py:23
  4.6 0.0 copy-start.5
  4.6 0.0 copy-start.3
  4.6 1.2 copy.15
  5.8 0.0 copy-done.5
  5.9 0.0 copy-start.6
  5.9 0.1 copy.17.pick_ref
  6.0 0.6 copy-done.6
  6.5 0.1 copy.18.weight_ref
  6.6 0.0 copy-done.3
  6.6 0.0 copy-start
  6.6 1.2 copy-done
  7.8 0.0 copy-start.1
  7.8 1.2 copy-done.1
  9.0 0.0 copy-start.2
  9.0 1.2 copy-done.2
  10.2 137.6 %shard_map.95 = bf16[1,8,5120]{2,1,0:T(8,128)(2,1)S(1)} custom-call(bf16[1,8,5120]{2,1,0:T(8,128)(2,1)S(1)} %copy-done.3, s32[1,8,6]{2,1,0:T(8,128)S(1)} %copy.17.pick_ref, f32[1,8,6]{2,1,0:T(8,128)S(1)} %copy.18.weight_ref, bf16[1,96,5120]{2,1,0:T(8,128)(2,1)S(1)} %copy-done, bf16[1,96,5120]{2,1,0:T(8,128)(2,1)S(1)} %copy-done.1, ...), custom_call_target="tpu_custom_call" | custom-call | tf_op jit(solution)/shard_map/pallas_call | solution.py:275
  147.8 0.2 fusion.8
  148.0 0.0 copy-start.4
  148.0 0.0 collective-permute-done
  148.1 0.9 copy-done.4
  149.0 0.3 fusion.3
  149.3 0.1 fusion.10
  149.4 0.3 convolution_convert_fusion
  149.7 0.8 copy.19
  150.5 0.6 copy.23
  (4 shorter events, 0.1 us)
Async XLA Ops:
  0.6 147.4 %collective-permute-start = (bf16[128,576]{0,1:T(8,128)(2,1)}, bf16[128,576]{0,1:T(8,128)(2,1)S(1)}, u32[]{:S(2)}, u32[]{:S(2)}) collective-permute-start(bf16[128,576]{0,1:T(8,128)(2,1)} %param.10), channel_id=1, source_target_pairs={{0,32},{32,64},{64,96},{96,128},{128,160},{160,192},{192,224},{224... | collective-permute-start | bytes 442376 | tf_op jit(solution)/shard_map/ppermute | solution.py:23
  4.6 1.2 copy-start.5
  4.6 2.0 %copy-start.3 = (bf16[1,8,5120]{2,1,0:T(8,128)(2,1)S(1)}, bf16[1,8,5120]{2,1,0:T(8,128)(2,1)}, u32[]{:S(2)}) copy-start(bf16[1,8,5120]{2,1,0:T(8,128)(2,1)} %tok_ref.1) | copy-start | bytes 245764
  5.9 0.7 copy-start.6
  6.6 1.2 copy-start
  7.8 1.2 copy-start.1
  9.0 1.2 copy-start.2
  148.0 0.9 copy-start.4

commit v2 on v0

v2 whole, which is shorter than its diff:
```python
import functools

import jax
import jax.numpy as jnp
from jax import lax
from jax.experimental import pallas as pl
from jax.experimental.pallas import tpu as pltpu
from jax.sharding import PartitionSpec as P

LATENT = 512
ROPE = 64
SCALE = 0.07216878364870322
NX = 4
NZ = 4
CAP = 2
MESH = pl.DeviceIdType.MESH
F32, BF16 = jnp.float32, jnp.bfloat16


def dot_nt(left, right):
    return lax.dot_general(left, right, (((1,), (1,)), ((), ())), preferred_element_type=F32)


def flat(ref):
    value = ref[...]
    return value.reshape(-1, value.shape[-1])


def moe_kernel(
    n_exp,
    tok_ref, pick_ref, weight_ref, q_ref, lat_ref, wg_ref, wu_ref, wd_ref, out_ref, att_ref,
    prev, tokens, table, own_table, thin_send, thin, wide_send, wide, chosen, gate_up, down_w, act,
    y_send, y_recv, mixed, final,
    local_sem, lat_s, lat_r, tok_s, tok_r, table_s, table_r, thin_s, thin_r, spread_s, spread_r, wide_s, wide_r,
    w_s, w_r, act_s, act_r, y_s, y_r, fin_s, fin_r,
):
    c, e = lax.axis_index("ctx"), lax.axis_index("exp")
    n_ctx = NX * NZ
    z, x = c // NX, c % NX
    tok, width = tok_ref.shape[1], tok_ref.shape[2]
    units, cols = wg_ref.shape[1], wd_ref.shape[1]
    chunk = NZ * CAP
    slots = n_exp * chunk
    half = width // 2
    part = half // NZ
    x_left, x_right, far = (x + NX - 1) % NX, (x + 1) % NX, (x + 2) % NX
    right, left = (z * NX + x_right, e), (z * NX + x_left, e)
    after, before = (lax.rem(c + 1, n_ctx), e), (lax.rem(c + n_ctx - 1, n_ctx), e)
    me = (c, e)

    def z_peer(d):
        return ((z + d) % NZ) * NX + x

    def at(ref, start, size, step):
        return ref.at[pl.ds(pl.multiple_of(start, step), size), :]

    def gate_of(index):
        return at(gate_up, index * 2 * units, units, units)

    def up_of(index):
        return at(gate_up, index * 2 * units + units, units, units)

    def down_of(index):
        return at(down_w, index * cols, cols, cols)

    def down_part(index, k):
        return at(down_w, index * cols + k * (cols // 2), cols // 2, cols // 2)

    def remote(src, dst, send, recv, peer):
        return pltpu.make_async_remote_copy(
            src_ref=src, dst_ref=dst, send_sem=send, recv_sem=recv, device_id=peer, device_id_type=MESH
        )

    own = [
        pltpu.make_async_copy(src.at[0], dst, local_sem.at[i])
        for i, (src, dst) in enumerate(((wg_ref, gate_of(x)), (wu_ref, up_of(x)), (wd_ref, down_of(x))))
    ]
    for copy in own:
        copy.start()

    barrier = pltpu.get_barrier_semaphore()
    for peer in [left, right, before, after] + [(z_peer(d), e) for d in range(1, NZ)]:
        pl.semaphore_signal(barrier, inc=1, device_id=peer, device_id_type=MESH)

    def greet(d, carry):
        pl.semaphore_signal(barrier, inc=1, device_id=(c, lax.rem(e + d, n_exp)), device_id_type=MESH)
        return carry

    lax.fori_loop(1, n_exp, greet, 0)

    lane = lax.broadcasted_iota(jnp.int32, (tok, slots), 1)
    lane_expert, inner = lane // chunk, lane % chunk
    picks, weights = pick_ref[0], weight_ref[0]
    named = jnp.zeros((tok, slots), F32)
    coef = jnp.zeros((tok, slots), F32)
    for k in range(picks.shape[1]):
        hit = picks[:, k : k + 1] == lane_expert
        named = jnp.where(hit, 1.0, named)
        coef = jnp.where(hit, weights[:, k : k + 1], coef)
    lower = lax.broadcasted_iota(jnp.int32, (tok, tok), 1) < lax.broadcasted_iota(jnp.int32, (tok, tok), 0)
    rank = jnp.dot(jnp.where(lower, 1.0, 0.0), named, preferred_element_type=F32)
    here = (inner // CAP == z) & (rank == (inner % CAP).astype(F32))
    own_table[0:tok, :] = jnp.where(here, coef, 0.0)
    own_table[tok : 2 * tok, :] = jnp.where(here, named, 0.0)
    taken = jnp.where(rank == (inner // NZ).astype(F32), named, 0.0)
    thin_pick = jnp.concatenate([jnp.where(inner % NZ == k, taken, 0.0) for k in range(NZ)], axis=0)
    thin_pick = jnp.transpose(thin_pick, (1, 0)).astype(BF16)
    first = tok_ref[0, :, 0:half].astype(F32)
    first = jnp.concatenate([first[:, k * part : (k + 1) * part] for k in range(NZ)], axis=0).astype(BF16)
    thin_send[...] = jnp.dot(thin_pick, first, preferred_element_type=F32).reshape(thin_send.shape).astype(BF16)

    own[0].wait()
    own[1].wait()
    pl.semaphore_wait(barrier, n_exp - 1 + NZ - 1 + 4)

    g_right = remote(gate_of(x), gate_of(x), w_s.at[0], w_r.at[0], right)
    u_right = remote(up_of(x), up_of(x), w_s.at[1], w_r.at[1], right)
    u_left = remote(up_of(x), up_of(x), w_s.at[2], w_r.at[2], left)
    g_left = remote(gate_of(x), gate_of(x), w_s.at[3], w_r.at[3], left)
    for copy in (g_right, u_left, u_right, g_left):
        copy.start()

    second = tok_ref.at[0, :, pl.ds(half, half)]
    for d in range(1, NZ):
        remote(own_table, table.at[z], table_s.at[d], table_r.at[z], (z_peer(d), e)).start()
        remote(second, tokens.at[z], tok_s.at[d], tok_r.at[z], (z_peer(d), e)).start()
    tokens[z] = tok_ref[0, :, half:width]
    table[z] = own_table[...]

    def thin_copy(peer):
        return remote(thin_send.at[peer], thin.at[e, z], thin_s, thin_r, (c, peer))

    def send_thin(d, carry):
        thin_copy(lax.rem(e + d, n_exp)).start()
        return carry

    pltpu.make_async_copy(thin_send.at[e], thin.at[e, z], thin_r).start()
    lax.fori_loop(1, n_exp, send_thin, 0)
    lat_copy = remote(lat_ref, prev, lat_s, lat_r, after)
    lat_copy.start()

    for d in range(1, NZ):
        p = (z + d) % NZ
        remote(own_table, table.at[p], table_s.at[d], table_r.at[p], me).wait_recv()
        remote(second, tokens.at[p], tok_s.at[d], tok_r.at[p], me).wait_recv()

    select = jnp.concatenate([table[i, tok : 2 * tok, :] for i in range(NZ)], axis=0)
    select = jnp.transpose(select, (1, 0)).astype(BF16)
    wide_send[...] = jnp.dot(select, flat(tokens), preferred_element_type=F32).reshape(wide_send.shape).astype(BF16)

    def send_wide(d, carry):
        peer = lax.rem(e + d, n_exp)
        remote(wide_send.at[peer], wide.at[e], wide_s, wide_r, (c, peer)).start()
        return carry

    pltpu.make_async_copy(wide_send.at[e], wide.at[e], wide_r).start()
    lax.fori_loop(1, n_exp, send_wide, 0)

    column = thin.at[:, z]
    remote(column, column, thin_s, thin_r, me).wait_recv()
    for d in range(1, NZ):
        remote(column, column, spread_s.at[d], spread_r.at[z], (z_peer(d), e)).start()

    lat_copy.wait_recv()
    n_att = lat_ref.shape[0]
    row = lax.broadcasted_iota(jnp.int32, (n_att, n_att), 0)
    col = lax.broadcasted_iota(jnp.int32, (n_att, n_att), 1)
    low = jnp.float32(-1e30)
    depth = LATENT + ROPE
    for h in range(q_ref.shape[1] // depth):
        query = q_ref[:, h * depth : (h + 1) * depth]
        s_own = jnp.where(col <= row, dot_nt(query, lat_ref[...]) * SCALE, low)
        s_prev = jnp.where(c > 0, dot_nt(query, prev[...]) * SCALE, low)
        top = jnp.maximum(jnp.max(s_own, axis=1, keepdims=True), jnp.max(s_prev, axis=1, keepdims=True))
        e_own, e_prev = jnp.exp(s_own - top), jnp.exp(s_prev - top)
        total = jnp.sum(e_own, axis=1, keepdims=True) + jnp.sum(e_prev, axis=1, keepdims=True)
        value = jnp.dot((e_own / total).astype(BF16), lat_ref[:, 0:LATENT], preferred_element_type=F32)
        value = value + jnp.dot((e_prev / total).astype(BF16), prev[:, 0:LATENT], preferred_element_type=F32)
        att_ref[:, h * LATENT : (h + 1) * LATENT] = value.astype(BF16)

    remote(gate_of(x_left), gate_of(x_left), w_s.at[0], w_r.at[0], me).wait_recv()
    g_on = remote(gate_of(x_left), gate_of(x_left), w_s.at[4], w_r.at[4], right)
    g_on.start()
    remote(up_of(x_right), up_of(x_right), w_s.at[2], w_r.at[2], me).wait_recv()
    u_on = remote(up_of(x_right), up_of(x_right), w_s.at[5], w_r.at[5], left)
    u_on.start()

    for d in range(1, NZ):
        p = (z + d) % NZ
        remote(thin.at[:, p], thin.at[:, p], spread_s.at[d], spread_r.at[p], me).wait_recv()
    block = NZ * chunk * NZ
    r_out = lax.broadcasted_iota(jnp.int32, (block, block), 0)
    r_in = lax.broadcasted_iota(jnp.int32, (block, block), 1)
    per = block // NZ
    sort = jnp.where(r_in == (r_out % per) * NZ + r_out // per, 1.0, 0.0).astype(BF16)

    def unfold(i, carry):
        piece = thin[pl.ds(i * NZ, NZ)].reshape(block, part)
        piece = jnp.dot(sort, piece, preferred_element_type=F32).astype(BF16)
        for k in range(NZ):
            chosen[pl.ds(pl.multiple_of(i * per, per), per), k * part : (k + 1) * part] = piece[k * per : (k + 1) * per]
        return carry

    lax.fori_loop(0, n_exp // NZ, unfold, 0)
    remote(wide, wide, wide_s, wide_r, me).wait_recv()
    chosen[:, half:width] = flat(wide)

    def activate(k, index):
        both = dot_nt(gate_up[pl.ds(pl.multiple_of(index * 2 * units, 2 * units), 2 * units), :], chosen[...])
        gate, upper = both[0:units], both[units : 2 * units]
        mine = at(act, (z * NX + index) * units, units, units)
        mine[...] = (gate / (1.0 + jnp.exp(-gate)) * upper).astype(BF16)
        for d in range(1, NZ):
            remote(mine, mine, act_s.at[k, d], act_r.at[k, z], (z_peer(d), e)).start()

    order = (x, x_left, x_right, far)
    activate(0, x)
    remote(up_of(x_left), up_of(x_left), w_s.at[1], w_r.at[1], me).wait_recv()
    activate(1, x_left)
    remote(gate_of(x_right), gate_of(x_right), w_s.at[3], w_r.at[3], me).wait_recv()
    activate(2, x_right)

    for copy in (g_right, u_right, u_left, g_left, g_on, u_on):
        copy.wait_send()
    own[2].wait()
    d_right = remote(down_of(x), down_of(x), w_s.at[6], w_r.at[6], right)
    d_left = remote(down_of(x), down_of(x), w_s.at[7], w_r.at[7], left)
    d_right.start()
    d_left.start()
    remote(gate_of(far), gate_of(far), w_s.at[4], w_r.at[4], me).wait_recv()
    remote(up_of(far), up_of(far), w_s.at[5], w_r.at[5], me).wait_recv()
    activate(3, far)
    for k in range(NX):
        for d in range(1, NZ):
            p = (z + d) % NZ
            theirs = at(act, (p * NX + order[k]) * units, units, units)
            remote(theirs, theirs, act_s.at[k, d], act_r.at[k, p], me).wait_recv()

    def project(k, index):
        y = jnp.dot(down_w[pl.ds(pl.multiple_of(index * cols, cols), cols), :], act[...], preferred_element_type=F32)
        y_send[k] = jnp.transpose(y, (1, 0)).reshape(y_send.shape[1:]).astype(BF16)

        def send_y(d, carry):
            peer = lax.rem(e + d, n_exp)
            remote(y_send.at[k, peer], y_recv.at[k, e], y_s.at[k], y_r.at[k], (c, peer)).start()
            return carry

        pltpu.make_async_copy(y_send.at[k, e], y_recv.at[k, e], y_r.at[k]).start()
        lax.fori_loop(1, n_exp, send_y, 0)

    combine = jnp.concatenate([table[i, 0:tok, :] for i in range(NZ)], axis=0)
    high = combine.astype(BF16)
    rest = (combine - high.astype(F32)).astype(BF16)

    def gather(k, index):
        remote(y_recv.at[k], y_recv.at[k], y_s.at[k], y_r.at[k], me).wait_recv()
        arrived = flat(y_recv.at[k])
        total = jnp.dot(high, arrived, preferred_element_type=F32)
        total = total + jnp.dot(rest, arrived, preferred_element_type=F32)
        mixed[k] = total.reshape(mixed.shape[1:]).astype(BF16)
        for d in range(1, NZ):
            p = (z + d) % NZ
            remote(mixed.at[k, p], final.at[z, index], fin_s.at[k, d], fin_r.at[k, z], (z_peer(d), e)).start()
        final[z, index] = mixed[k, z]

    project(0, x)
    remote(down_of(x_left), down_of(x_left), w_s.at[6], w_r.at[6], me).wait_recv()
    f_right = remote(down_part(x_left, 0), down_part(x_left, 0), w_s.at[8], w_r.at[8], right)
    f_right.start()
    remote(down_of(x_right), down_of(x_right), w_s.at[7], w_r.at[7], me).wait_recv()
    f_left = remote(down_part(x_right, 1), down_part(x_right, 1), w_s.at[9], w_r.at[9], left)
    f_left.start()
    project(1, x_left)
    project(2, x_right)
    gather(0, x)
    remote(down_part(far, 0), down_part(far, 0), w_s.at[8], w_r.at[8], me).wait_recv()
    remote(down_part(far, 1), down_part(far, 1), w_s.at[9], w_r.at[9], me).wait_recv()
    project(3, far)
    gather(1, x_left)
    gather(2, x_right)
    gather(3, far)
    for k in range(NX):
        for d in range(1, NZ):
            p = (z + d) % NZ
            remote(mixed.at[k, p], final.at[p, order[k]], fin_s.at[k, d], fin_r.at[k, p], me).wait_recv()
    pieces = [final[i // NX, i % NX].astype(F32) for i in range(n_ctx)]
    out_ref[0] = jnp.concatenate(pieces, axis=1).astype(BF16)

    lat_copy.wait_send()
    for d in range(1, NZ):
        remote(own_table, table.at[z], table_s.at[d], table_r.at[z], me).wait_send()
        remote(second, tokens.at[z], tok_s.at[d], tok_r.at[z], me).wait_send()
        remote(column, column, spread_s.at[d], spread_r.at[z], me).wait_send()
        for k in range(NX):
            mine = at(act, (z * NX + order[k]) * units, units, units)
            remote(mine, mine, act_s.at[k, d], act_r.at[k, z], me).wait_send()
            remote(mixed.at[k, 0], final.at[z, 0], fin_s.at[k, d], fin_r.at[k, z], me).wait_send()
    for copy in (d_right, d_left, f_right, f_left):
        copy.wait_send()
    others = pl.ds(0, n_exp - 1)
    remote(thin_send.at[others], thin_send.at[others], thin_s, thin_r, me).wait_send()
    remote(wide_send.at[others], wide_send.at[others], wide_s, wide_r, me).wait_send()
    for k in range(NX):
        remote(y_send.at[k, others], y_send.at[k, others], y_s.at[k], y_r.at[k], me).wait_send()


def on_device(hidden, queries, latents, expert_ids, route_weight, w_gate, w_up, w_down):
    n_exp = lax.axis_size("exp")
    tok, width = hidden.shape[1:]
    units, hid = w_gate.shape[1], w_down.shape[2]
    cols = w_down.shape[1]
    chunk = NZ * CAP
    slots = n_exp * chunk
    half = width // 2
    heads = queries.shape[1] // (LATENT + ROPE)
    dma = pltpu.SemaphoreType.DMA
    vmem = pl.BlockSpec(memory_space=pltpu.VMEM)
    hbm = pl.BlockSpec(memory_space=pltpu.HBM)
    moe_out, attended = pl.pallas_call(
        functools.partial(moe_kernel, n_exp),
        out_shape=(
            jax.ShapeDtypeStruct(hidden.shape, BF16),
            jax.ShapeDtypeStruct((queries.shape[0], heads * LATENT), BF16),
        ),
        in_specs=[vmem, vmem, vmem, vmem, vmem, hbm, hbm, hbm],
        out_specs=(vmem, vmem),
        scratch_shapes=[
            pltpu.VMEM(latents.shape, BF16),
            pltpu.VMEM((NZ, tok, half), BF16),
            pltpu.VMEM((NZ, 2 * tok, slots), F32),
            pltpu.VMEM((2 * tok, slots), F32),
            pltpu.VMEM((n_exp, chunk, half // NZ), BF16),
            pltpu.VMEM((n_exp, NZ, chunk, half // NZ), BF16),
            pltpu.VMEM((n_exp, chunk, half), BF16),
            pltpu.VMEM((n_exp, chunk, half), BF16),
            pltpu.VMEM((slots, width), BF16),
            pltpu.VMEM((NX * 2 * units, width), BF16),
            pltpu.VMEM((NX * cols, hid), BF16),
            pltpu.VMEM((NZ * NX * units, slots), BF16),
            pltpu.VMEM((NX, n_exp, chunk, cols), BF16),
            pltpu.VMEM((NX, n_exp, chunk, cols), BF16),
            pltpu.VMEM((NX, NZ, tok, cols), BF16),
            pltpu.VMEM((NZ, NX, tok, cols), BF16),
            dma((3,)),
            dma, dma,
            dma((NZ,)), dma((NZ,)), dma((NZ,)), dma((NZ,)),
            dma, dma,
            dma((NZ,)), dma((NZ,)),
            dma, dma,
            dma((10,)), dma((10,)),
            dma((NX, NZ)), dma((NX, NZ)),
            dma((NX,)), dma((NX,)),
            dma((NX, NZ)), dma((NX, NZ)),
        ],
        compiler_params=pltpu.CompilerParams(
            collective_id=0, has_side_effects=True, vmem_limit_bytes=56 << 20
        ),
    )(hidden, expert_ids, route_weight, queries, latents, w_gate, w_up, w_down)
    return attended, moe_out


def solution(mesh):
    placed = (
        P("exp", "ctx", None),
        P("ctx", "exp"),
        P("ctx", None),
        P("exp", "ctx", None),
        P("exp", "ctx", None),
        P("exp", "ctx", None),
        P("exp", "ctx", None),
        P("exp", "ctx", None),
    )
    return jax.shard_map(
        on_device,
        mesh=mesh,
        in_specs=placed,
        out_specs=(P("ctx", "exp"), P("exp", "ctx", None)),
        check_vma=False,
    )
```

time: 343 us -> 139 us (0.41)
  waiting for transfers between devices: 252 us -> 0 us
  Pallas kernels: 0 us -> 131 us
  blocking collectives: 29.4 us -> 0 us
  starting transfers between devices: 19.7 us -> 0 us
  matrix products: 18.2 us -> 0 us
  between operations: 14.2 us -> 0.66 us
    all_gather x2 -> x0, waiting for transfers between devices: 218 us -> none  [the longest x1 126 us: on_device(): lax.all_gather(arrived.reshape(slots, width), 'ctx', axis=0, tiled=True)]
    pallas_call x0 -> x1, Pallas kernels: none -> 131 us  [on_device(): pl.pallas_call(functools.partial(moe_kernel, n_exp), out_shape=(jax.Shape...]
    all_to_all x2 -> x0, waiting for transfers between devices: 34.9 us -> none  [the longest x1 18 us: on_device(): lax.all_to_all(columns, 'ctx', split_axis=0, concat_axis=3, tiled=True)]
    all_to_all x1 -> x0, blocking collectives: 29.4 us -> none  [on_device(): lax.all_to_all(outgoing, 'exp', split_axis=0, concat_axis=0, tiled=True)]
    dot_general x8 -> x0, matrix products: 18.2 us -> none  [the longest x3 14.8 us: times_rows(): lax.dot_general(left, right, (((1,), (1,)), ((), ())), preferred_element_...]
    all_to_all x2 -> x0, starting transfers between devices: 16.3 us -> none  [the longest x1 10.3 us: on_device(): lax.all_to_all(by_block, 'exp', split_axis=1, concat_axis=1, tiled=True)]
    unnamed x17 -> x9, local copies, waits for them, and re-layouts: 2.12 us -> 6.08 us
  transfers between devices with their start and end apart: 5 -> 0, of which waited for: 4 -> 0; matrix products, arithmetic and copies ran while one was open for 1% -> 0% of each run, Pallas kernels for 0% -> 0%
where the time goes in v2:
time: 139 us; the launch traced here: 138 us
  Pallas kernels  131 us (94%)
  local copies, waits for them, and re-layouts  6.08 us (4%)
    pallas_call x1, Pallas kernels, on_device(): pl.pallas_call(functools.partial(moe_kernel, n_exp), out_shape=(jax.Shape...  131 us
    unnamed x9, local copies, waits for them, and re-layouts  6.08 us

profile of v2, /device:TPU:1, one launch (start us, length us, event | category | flops | bytes accessed | tf_op | source)
XLA Modules:
  0.0 138.1 jit_solution(4373256952866660742)
XLA Ops:
  0.6 0.0 copy-start.1
  0.6 1.4 copy.10.pick_ref
  2.0 0.0 copy-done.1
  2.0 0.7 copy.11.weight_ref
  2.7 1.7 %copy.12.lat_ref = bf16[128,576]{1,0:T(8,128)(2,1)} copy(bf16[128,576]{0,1:T(8,128)(2,1)} %param.10) | data formatting | bytes 294912 | tf_op args[2]
  4.4 131.4 %shard_map.95 = (bf16[1,8,5120]{2,1,0:T(8,128)(2,1)}, bf16[128,1024]{1,0:T(8,128)(2,1)}) custom-call(bf16[1,8,5120]{2,1,0:T(8,128)(2,1)} %tok_ref.1, s32[1,8,6]{2,1,0:T(8,128)} %copy.10.pick_ref, f32[1,8,6]{2,1,0:T(8,128)} %copy.11.weight_ref, bf16[128,1152]{1,0:T(8,128)(2,1)} %q_ref.1, bf16[128,576]{1,0:T(8,128)(2,1)} %copy.12.lat_ref, ...), custom_call_target="tpu_custom_call" | custom-call | tf_op jit(solution)/shard_map/pallas_call | solution.py:319
  135.8 0.0 copy-start
  135.8 1.7 %copy.15 = bf16[128,1024]{1,0:T(8,128)(2,1)} copy(bf16[128,1024]{1,0:T(8,128)(2,1)} %get-tuple-element.8) | data formatting | bytes 524288
  137.5 0.0 copy-done
  137.5 0.6 copy.16
Async XLA Ops:
  0.6 1.4 copy-start.1
  135.8 1.7 %copy-start = (bf16[1,8,5120]{2,1,0:T(8,128)(2,1)S(1)}, bf16[1,8,5120]{2,1,0:T(8,128)(2,1)}, u32[]{:S(2)}) copy-start(bf16[1,8,5120]{2,1,0:T(8,128)(2,1)} %get-tuple-element.9) | copy-start | bytes 245764

commit v3 on v2

--- a/solution.py
+++ b/solution.py
@@ -88,23 +88,21 @@
 
     lax.fori_loop(1, n_exp, greet, 0)
 
-    lane = lax.broadcasted_iota(jnp.int32, (tok, slots), 1)
-    lane_expert, inner = lane // chunk, lane % chunk
-    picks, weights = pick_ref[0], weight_ref[0]
-    named = jnp.zeros((tok, slots), F32)
-    coef = jnp.zeros((tok, slots), F32)
-    for k in range(picks.shape[1]):
-        hit = picks[:, k : k + 1] == lane_expert
+    slot = lax.broadcasted_iota(jnp.int32, (slots, tok), 0)
+    slot_expert, inner = slot // chunk, slot % chunk
+    named = jnp.zeros((slots, tok), F32)
+    coef = jnp.zeros((slots, tok), F32)
+    for k in range(pick_ref.shape[0]):
+        hit = pick_ref[k] == slot_expert
         named = jnp.where(hit, 1.0, named)
-        coef = jnp.where(hit, weights[:, k : k + 1], coef)
-    lower = lax.broadcasted_iota(jnp.int32, (tok, tok), 1) < lax.broadcasted_iota(jnp.int32, (tok, tok), 0)
-    rank = jnp.dot(jnp.where(lower, 1.0, 0.0), named, preferred_element_type=F32)
+        coef = jnp.where(hit, weight_ref[k], coef)
+    upper = lax.broadcasted_iota(jnp.int32, (tok, tok), 0) < lax.broadcasted_iota(jnp.int32, (tok, tok), 1)
+    rank = jnp.dot(named, jnp.where(upper, 1.0, 0.0), preferred_element_type=F32)
     here = (inner // CAP == z) & (rank == (inner % CAP).astype(F32))
-    own_table[0:tok, :] = jnp.where(here, coef, 0.0)
-    own_table[tok : 2 * tok, :] = jnp.where(here, named, 0.0)
+    both = jnp.concatenate([jnp.where(here, coef, 0.0), jnp.where(here, named, 0.0)], axis=1)
+    own_table[...] = jnp.transpose(both, (1, 0))
     taken = jnp.where(rank == (inner // NZ).astype(F32), named, 0.0)
-    thin_pick = jnp.concatenate([jnp.where(inner % NZ == k, taken, 0.0) for k in range(NZ)], axis=0)
-    thin_pick = jnp.transpose(thin_pick, (1, 0)).astype(BF16)
+    thin_pick = jnp.concatenate([jnp.where(inner % NZ == k, taken, 0.0) for k in range(NZ)], axis=1).astype(BF16)
     first = tok_ref[0, :, 0:half].astype(F32)
     first = jnp.concatenate([first[:, k * part : (k + 1) * part] for k in range(NZ)], axis=0).astype(BF16)
     thin_send[...] = jnp.dot(thin_pick, first, preferred_element_type=F32).reshape(thin_send.shape).astype(BF16)
@@ -158,25 +156,38 @@
 
     column = thin.at[:, z]
     remote(column, column, thin_s, thin_r, me).wait_recv()
-    for d in range(1, NZ):
-        remote(column, column, spread_s.at[d], spread_r.at[z], (z_peer(d), e)).start()
+    for d in (1, NZ - 1):
+        remote(column, column, spread_s.at[d], spread_r.at[d], (z_peer(d), e)).start()
 
     lat_copy.wait_recv()
-    n_att = lat_ref.shape[0]
+    n_att = lat_ref.shape[1]
     row = lax.broadcasted_iota(jnp.int32, (n_att, n_att), 0)
     col = lax.broadcasted_iota(jnp.int32, (n_att, n_att), 1)
     low = jnp.float32(-1e30)
     depth = LATENT + ROPE
     for h in range(q_ref.shape[1] // depth):
         query = q_ref[:, h * depth : (h + 1) * depth]
-        s_own = jnp.where(col <= row, dot_nt(query, lat_ref[...]) * SCALE, low)
-        s_prev = jnp.where(c > 0, dot_nt(query, prev[...]) * SCALE, low)
+        s_own = jnp.where(col <= row, jnp.dot(query, lat_ref[...], preferred_element_type=F32) * SCALE, low)
+        s_prev = jnp.where(c > 0, jnp.dot(query, prev[...], preferred_element_type=F32) * SCALE, low)
         top = jnp.maximum(jnp.max(s_own, axis=1, keepdims=True), jnp.max(s_prev, axis=1, keepdims=True))
         e_own, e_prev = jnp.exp(s_own - top), jnp.exp(s_prev - top)
         total = jnp.sum(e_own, axis=1, keepdims=True) + jnp.sum(e_prev, axis=1, keepdims=True)
-        value = jnp.dot((e_own / total).astype(BF16), lat_ref[:, 0:LATENT], preferred_element_type=F32)
-        value = value + jnp.dot((e_prev / total).astype(BF16), prev[:, 0:LATENT], preferred_element_type=F32)
+        value = dot_nt((e_own / total).astype(BF16), lat_ref[0:LATENT, :])
+        value = value + dot_nt((e_prev / total).astype(BF16), prev[0:LATENT, :])
         att_ref[:, h * LATENT : (h + 1) * LATENT] = value.astype(BF16)
+
+    z_down, z_up, z_far = (z + NZ - 1) % NZ, (z + 1) % NZ, (z + 2) % NZ
+    above, below = (z_peer(1), e), (z_peer(NZ - 1), e)
+
+    def thin_half(index, k):
+        return thin.at[pl.ds(k * (n_exp // 2), n_exp // 2), index]
+
+    remote(thin.at[:, z_down], thin.at[:, z_down], spread_s.at[1], spread_r.at[1], me).wait_recv()
+    t_up = remote(thin_half(z_down, 0), thin_half(z_down, 0), spread_s.at[0], spread_r.at[0], above)
+    t_up.start()
+    remote(thin.at[:, z_up], thin.at[:, z_up], spread_s.at[3], spread_r.at[3], me).wait_recv()
+    t_down = remote(thin_half(z_up, 1), thin_half(z_up, 1), spread_s.at[2], spread_r.at[2], below)
+    t_down.start()
 
     remote(gate_of(x_left), gate_of(x_left), w_s.at[0], w_r.at[0], me).wait_recv()
     g_on = remote(gate_of(x_left), gate_of(x_left), w_s.at[4], w_r.at[4], right)
@@ -185,9 +196,8 @@
     u_on = remote(up_of(x_right), up_of(x_right), w_s.at[5], w_r.at[5], left)
     u_on.start()
 
-    for d in range(1, NZ):
-        p = (z + d) % NZ
-        remote(thin.at[:, p], thin.at[:, p], spread_s.at[d], spread_r.at[p], me).wait_recv()
+    remote(thin_half(z_far, 0), thin_half(z_far, 0), spread_s.at[0], spread_r.at[0], me).wait_recv()
+    remote(thin_half(z_far, 1), thin_half(z_far, 1), spread_s.at[2], spread_r.at[2], me).wait_recv()
     block = NZ * chunk * NZ
     r_out = lax.broadcasted_iota(jnp.int32, (block, block), 0)
     r_in = lax.broadcasted_iota(jnp.int32, (block, block), 1)
@@ -210,8 +220,20 @@
         gate, upper = both[0:units], both[units : 2 * units]
         mine = at(act, (z * NX + index) * units, units, units)
         mine[...] = (gate / (1.0 + jnp.exp(-gate)) * upper).astype(BF16)
-        for d in range(1, NZ):
-            remote(mine, mine, act_s.at[k, d], act_r.at[k, z], (z_peer(d), e)).start()
+        remote(mine, mine, act_s.at[k, 1], act_r.at[k, 1], above).start()
+        remote(mine, mine, act_s.at[k, 3], act_r.at[k, 3], below).start()
+
+    def act_of(z_index, k):
+        return at(act, (z_index * NX + order[k]) * units, units, units)
+
+    def act_half(z_index, k, j):
+        return at(act, (z_index * NX + order[k]) * units + j * (units // 2), units // 2, units // 2)
+
+    def pass_on(k):
+        remote(act_of(z_down, k), act_of(z_down, k), act_s.at[k, 1], act_r.at[k, 1], me).wait_recv()
+        remote(act_half(z_down, k, 0), act_half(z_down, k, 0), act_s.at[k, 0], act_r.at[k, 0], above).start()
+        remote(act_of(z_up, k), act_of(z_up, k), act_s.at[k, 3], act_r.at[k, 3], me).wait_recv()
+        remote(act_half(z_up, k, 1), act_half(z_up, k, 1), act_s.at[k, 2], act_r.at[k, 2], below).start()
 
     order = (x, x_left, x_right, far)
     activate(0, x)
@@ -219,6 +241,8 @@
     activate(1, x_left)
     remote(gate_of(x_right), gate_of(x_right), w_s.at[3], w_r.at[3], me).wait_recv()
     activate(2, x_right)
+    for k in range(3):
+        pass_on(k)
 
     for copy in (g_right, u_right, u_left, g_left, g_on, u_on):
         copy.wait_send()
@@ -230,11 +254,10 @@
     remote(gate_of(far), gate_of(far), w_s.at[4], w_r.at[4], me).wait_recv()
     remote(up_of(far), up_of(far), w_s.at[5], w_r.at[5], me).wait_recv()
     activate(3, far)
+    pass_on(3)
     for k in range(NX):
-        for d in range(1, NZ):
-            p = (z + d) % NZ
-            theirs = at(act, (p * NX + order[k]) * units, units, units)
-            remote(theirs, theirs, act_s.at[k, d], act_r.at[k, p], me).wait_recv()
+        remote(act_half(z_far, k, 0), act_half(z_far, k, 0), act_s.at[k, 0], act_r.at[k, 0], me).wait_recv()
+        remote(act_half(z_far, k, 1), act_half(z_far, k, 1), act_s.at[k, 2], act_r.at[k, 2], me).wait_recv()
 
     def project(k, index):
         y = jnp.dot(down_w[pl.ds(pl.multiple_of(index * cols, cols), cols), :], act[...], preferred_element_type=F32)
@@ -290,13 +313,15 @@
     for d in range(1, NZ):
         remote(own_table, table.at[z], table_s.at[d], table_r.at[z], me).wait_send()
         remote(second, tokens.at[z], tok_s.at[d], tok_r.at[z], me).wait_send()
-        remote(column, column, spread_s.at[d], spread_r.at[z], me).wait_send()
         for k in range(NX):
-            mine = at(act, (z * NX + order[k]) * units, units, units)
-            remote(mine, mine, act_s.at[k, d], act_r.at[k, z], me).wait_send()
             remote(mixed.at[k, 0], final.at[z, 0], fin_s.at[k, d], fin_r.at[k, z], me).wait_send()
-    for copy in (d_right, d_left, f_right, f_left):
+    for copy in (d_right, d_left, f_right, f_left, t_up, t_down):
         copy.wait_send()
+    for d in (1, NZ - 1):
+        remote(column, column, spread_s.at[d], spread_r.at[d], me).wait_send()
+    for k in range(NX):
+        for j, part_of in ((1, act_of(z, k)), (3, act_of(z, k)), (0, act_half(z_down, k, 0)), (2, act_half(z_up, k, 1))):
+            remote(part_of, part_of, act_s.at[k, j], act_r.at[k, j], me).wait_send()
     others = pl.ds(0, n_exp - 1)
     remote(thin_send.at[others], thin_send.at[others], thin_s, thin_r, me).wait_send()
     remote(wide_send.at[others], wide_send.at[others], wide_s, wide_r, me).wait_send()
@@ -325,7 +350,7 @@
         in_specs=[vmem, vmem, vmem, vmem, vmem, hbm, hbm, hbm],
         out_specs=(vmem, vmem),
         scratch_shapes=[
-            pltpu.VMEM(latents.shape, BF16),
+            pltpu.VMEM(latents.shape[::-1], BF16),
             pltpu.VMEM((NZ, tok, half), BF16),
             pltpu.VMEM((NZ, 2 * tok, slots), F32),
             pltpu.VMEM((2 * tok, slots), F32),
@@ -355,7 +380,7 @@
         compiler_params=pltpu.CompilerParams(
             collective_id=0, has_side_effects=True, vmem_limit_bytes=56 << 20
         ),
-    )(hidden, expert_ids, route_weight, queries, latents, w_gate, w_up, w_down)
+    )(hidden, jnp.transpose(expert_ids, (2, 0, 1)), jnp.transpose(route_weight, (2, 0, 1)), queries, latents.T, w_gate, w_up, w_down)
     return attended, moe_out
 
 

time: 139 us -> 135 us (0.971)
  local copies, waits for them, and re-layouts: 6.08 us -> 2.34 us
    unnamed x9 -> x4, local copies, waits for them, and re-layouts: 6.08 us -> 2.34 us
where the time goes in v3:
time: 135 us
  Pallas kernels  132 us (98%)
  local copies, waits for them, and re-layouts  2.34 us (2%)
    pallas_call x1, Pallas kernels, on_device(): pl.pallas_call(functools.partial(moe_kernel, n_exp), out_shape=(jax.Shape...  132 us

profile of v3, /device:TPU:1, one launch (start us, length us, event | category | flops | bytes accessed | tf_op | source)
XLA Modules:
  0.0 135.0 jit_solution(18263998110279404389)
XLA Ops:
  0.6 132.0 %shard_map.95 = (bf16[1,8,5120]{2,1,0:T(8,128)(2,1)}, bf16[128,1024]{1,0:T(8,128)(2,1)}) custom-call(bf16[1,8,5120]{2,1,0:T(8,128)(2,1)} %tok_ref.1, s32[6,1,8]{2,1,0:T(1,128)} %bitcast.4, f32[6,1,8]{2,1,0:T(1,128)} %bitcast.5, bf16[128,1152]{1,0:T(8,128)(2,1)} %q_ref.1, bf16[576,128]{1,0:T(8,128)(2,1)} %bitcast.3, bf16[1,96,5120]{2,1,0:T(8,128)(2,1)} %wg_ref.1, ...), custom_call_target="tpu_custom_call" | custom-call | tf_op jit(solution)/shard_map/pallas_call | solution.py:344
  132.6 0.0 copy-start
  132.6 1.7 %copy.12 = bf16[128,1024]{1,0:T(8,128)(2,1)} copy(bf16[128,1024]{1,0:T(8,128)(2,1)} %get-tuple-element.8) | data formatting | bytes 524288
  134.3 0.0 copy-done
  134.3 0.6 copy.13
Async XLA Ops:
  132.6 1.7 %copy-start = (bf16[1,8,5120]{2,1,0:T(8,128)(2,1)S(1)}, bf16[1,8,5120]{2,1,0:T(8,128)(2,1)}, u32[]{:S(2)}) copy-start(bf16[1,8,5120]{2,1,0:T(8,128)(2,1)} %get-tuple-element.9) | copy-start | bytes 245764

commit v4 on v3

--- a/solution.py
+++ b/solution.py
@@ -41,8 +41,8 @@
     units, cols = wg_ref.shape[1], wd_ref.shape[1]
     chunk = NZ * CAP
     slots = n_exp * chunk
-    half = width // 2
-    part = half // NZ
+    part = thin.shape[-1]
+    half = part * NZ
     x_left, x_right, far = (x + NX - 1) % NX, (x + 1) % NX, (x + 2) % NX
     right, left = (z * NX + x_right, e), (z * NX + x_left, e)
     after, before = (lax.rem(c + 1, n_ctx), e), (lax.rem(c + n_ctx - 1, n_ctx), e)
@@ -118,7 +118,7 @@
     for copy in (g_right, u_left, u_right, g_left):
         copy.start()
 
-    second = tok_ref.at[0, :, pl.ds(half, half)]
+    second = tok_ref.at[0, :, pl.ds(half, width - half)]
     for d in range(1, NZ):
         remote(own_table, table.at[z], table_s.at[d], table_r.at[z], (z_peer(d), e)).start()
         remote(second, tokens.at[z], tok_s.at[d], tok_r.at[z], (z_peer(d), e)).start()
@@ -158,6 +158,34 @@
     remote(column, column, thin_s, thin_r, me).wait_recv()
     for d in (1, NZ - 1):
         remote(column, column, spread_s.at[d], spread_r.at[d], (z_peer(d), e)).start()
+
+    remote(gate_of(x_left), gate_of(x_left), w_s.at[0], w_r.at[0], me).wait_recv()
+    g_on = remote(gate_of(x_left), gate_of(x_left), w_s.at[4], w_r.at[4], right)
+    g_on.start()
+    remote(up_of(x_right), up_of(x_right), w_s.at[2], w_r.at[2], me).wait_recv()
+    u_on = remote(up_of(x_right), up_of(x_right), w_s.at[5], w_r.at[5], left)
+    u_on.start()
+
+    own[2].wait()
+    d_right = remote(down_part(x, 0), down_part(x, 0), w_s.at[6], w_r.at[6], right)
+    d_left = remote(down_part(x, 1), down_part(x, 1), w_s.at[7], w_r.at[7], left)
+    d_right_too = remote(down_part(x, 1), down_part(x, 1), w_s.at[10], w_r.at[10], right)
+    d_left_too = remote(down_part(x, 0), down_part(x, 0), w_s.at[11], w_r.at[11], left)
+    for copy in (d_right, d_left, d_right_too, d_left_too):
+        copy.start()
+
+    z_down, z_up, z_far = (z + NZ - 1) % NZ, (z + 1) % NZ, (z + 2) % NZ
+    above, below = (z_peer(1), e), (z_peer(NZ - 1), e)
+
+    def thin_half(index, k):
+        return thin.at[pl.ds(k * (n_exp // 2), n_exp // 2), index]
+
+    remote(thin.at[:, z_down], thin.at[:, z_down], spread_s.at[1], spread_r.at[1], me).wait_recv()
+    t_up = remote(thin_half(z_down, 0), thin_half(z_down, 0), spread_s.at[0], spread_r.at[0], above)
+    t_up.start()
+    remote(thin.at[:, z_up], thin.at[:, z_up], spread_s.at[3], spread_r.at[3], me).wait_recv()
+    t_down = remote(thin_half(z_up, 1), thin_half(z_up, 1), spread_s.at[2], spread_r.at[2], below)
+    t_down.start()
 
     lat_copy.wait_recv()
     n_att = lat_ref.shape[1]
@@ -176,26 +204,6 @@
         value = value + dot_nt((e_prev / total).astype(BF16), prev[0:LATENT, :])
         att_ref[:, h * LATENT : (h + 1) * LATENT] = value.astype(BF16)
 
-    z_down, z_up, z_far = (z + NZ - 1) % NZ, (z + 1) % NZ, (z + 2) % NZ
-    above, below = (z_peer(1), e), (z_peer(NZ - 1), e)
-
-    def thin_half(index, k):
-        return thin.at[pl.ds(k * (n_exp // 2), n_exp // 2), index]
-
-    remote(thin.at[:, z_down], thin.at[:, z_down], spread_s.at[1], spread_r.at[1], me).wait_recv()
-    t_up = remote(thin_half(z_down, 0), thin_half(z_down, 0), spread_s.at[0], spread_r.at[0], above)
-    t_up.start()
-    remote(thin.at[:, z_up], thin.at[:, z_up], spread_s.at[3], spread_r.at[3], me).wait_recv()
-    t_down = remote(thin_half(z_up, 1), thin_half(z_up, 1), spread_s.at[2], spread_r.at[2], below)
-    t_down.start()
-
-    remote(gate_of(x_left), gate_of(x_left), w_s.at[0], w_r.at[0], me).wait_recv()
-    g_on = remote(gate_of(x_left), gate_of(x_left), w_s.at[4], w_r.at[4], right)
-    g_on.start()
-    remote(up_of(x_right), up_of(x_right), w_s.at[2], w_r.at[2], me).wait_recv()
-    u_on = remote(up_of(x_right), up_of(x_right), w_s.at[5], w_r.at[5], left)
-    u_on.start()
-
     remote(thin_half(z_far, 0), thin_half(z_far, 0), spread_s.at[0], spread_r.at[0], me).wait_recv()
     remote(thin_half(z_far, 1), thin_half(z_far, 1), spread_s.at[2], spread_r.at[2], me).wait_recv()
     block = NZ * chunk * NZ
@@ -244,17 +252,16 @@
     for k in range(3):
         pass_on(k)
 
-    for copy in (g_right, u_right, u_left, g_left, g_on, u_on):
-        copy.wait_send()
-    own[2].wait()
-    d_right = remote(down_of(x), down_of(x), w_s.at[6], w_r.at[6], right)
-    d_left = remote(down_of(x), down_of(x), w_s.at[7], w_r.at[7], left)
-    d_right.start()
-    d_left.start()
     remote(gate_of(far), gate_of(far), w_s.at[4], w_r.at[4], me).wait_recv()
     remote(up_of(far), up_of(far), w_s.at[5], w_r.at[5], me).wait_recv()
     activate(3, far)
     pass_on(3)
+    remote(down_part(x_left, 0), down_part(x_left, 0), w_s.at[6], w_r.at[6], me).wait_recv()
+    f_right = remote(down_part(x_left, 0), down_part(x_left, 0), w_s.at[8], w_r.at[8], right)
+    f_right.start()
+    remote(down_part(x_right, 1), down_part(x_right, 1), w_s.at[7], w_r.at[7], me).wait_recv()
+    f_left = remote(down_part(x_right, 1), down_part(x_right, 1), w_s.at[9], w_r.at[9], left)
+    f_left.start()
     for k in range(NX):
         remote(act_half(z_far, k, 0), act_half(z_far, k, 0), act_s.at[k, 0], act_r.at[k, 0], me).wait_recv()
         remote(act_half(z_far, k, 1), act_half(z_far, k, 1), act_s.at[k, 2], act_r.at[k, 2], me).wait_recv()
@@ -287,18 +294,14 @@
         final[z, index] = mixed[k, z]
 
     project(0, x)
-    remote(down_of(x_left), down_of(x_left), w_s.at[6], w_r.at[6], me).wait_recv()
-    f_right = remote(down_part(x_left, 0), down_part(x_left, 0), w_s.at[8], w_r.at[8], right)
-    f_right.start()
-    remote(down_of(x_right), down_of(x_right), w_s.at[7], w_r.at[7], me).wait_recv()
-    f_left = remote(down_part(x_right, 1), down_part(x_right, 1), w_s.at[9], w_r.at[9], left)
-    f_left.start()
+    remote(down_part(x_left, 1), down_part(x_left, 1), w_s.at[10], w_r.at[10], me).wait_recv()
     project(1, x_left)
+    remote(down_part(x_right, 0), down_part(x_right, 0), w_s.at[11], w_r.at[11], me).wait_recv()
     project(2, x_right)
-    gather(0, x)
     remote(down_part(far, 0), down_part(far, 0), w_s.at[8], w_r.at[8], me).wait_recv()
     remote(down_part(far, 1), down_part(far, 1), w_s.at[9], w_r.at[9], me).wait_recv()
     project(3, far)
+    gather(0, x)
     gather(1, x_left)
     gather(2, x_right)
     gather(3, far)
@@ -315,7 +318,7 @@
         remote(second, tokens.at[z], tok_s.at[d], tok_r.at[z], me).wait_send()
         for k in range(NX):
             remote(mixed.at[k, 0], final.at[z, 0], fin_s.at[k, d], fin_r.at[k, z], me).wait_send()
-    for copy in (d_right, d_left, f_right, f_left, t_up, t_down):
+    for copy in (g_right, u_right, u_left, g_left, g_on, u_on, d_right, d_left, d_right_too, d_left_too, f_right, f_left, t_up, t_down):
         copy.wait_send()
     for d in (1, NZ - 1):
         remote(column, column, spread_s.at[d], spread_r.at[d], me).wait_send()
@@ -351,13 +354,13 @@
         out_specs=(vmem, vmem),
         scratch_shapes=[
             pltpu.VMEM(latents.shape[::-1], BF16),
-            pltpu.VMEM((NZ, tok, half), BF16),
+            pltpu.VMEM((NZ, tok, width - half), BF16),
             pltpu.VMEM((NZ, 2 * tok, slots), F32),
             pltpu.VMEM((2 * tok, slots), F32),
             pltpu.VMEM((n_exp, chunk, half // NZ), BF16),
             pltpu.VMEM((n_exp, NZ, chunk, half // NZ), BF16),
-            pltpu.VMEM((n_exp, chunk, half), BF16),
-            pltpu.VMEM((n_exp, chunk, half), BF16),
+            pltpu.VMEM((n_exp, chunk, width - half), BF16),
+            pltpu.VMEM((n_exp, chunk, width - half), BF16),
             pltpu.VMEM((slots, width), BF16),
             pltpu.VMEM((NX * 2 * units, width), BF16),
             pltpu.VMEM((NX * cols, hid), BF16),
@@ -372,7 +375,7 @@
             dma, dma,
             dma((NZ,)), dma((NZ,)),
             dma, dma,
-            dma((10,)), dma((10,)),
+            dma((12,)), dma((12,)),
             dma((NX, NZ)), dma((NX, NZ)),
             dma((NX,)), dma((NX,)),
             dma((NX, NZ)), dma((NX, NZ)),

time: 135 us -> 133 us (0.985)
  Pallas kernels: 132 us -> 130 us
    pallas_call x1, Pallas kernels: 132 us -> 130 us  [on_device(): pl.pallas_call(functools.partial(moe_kernel, n_exp), out_shape=(jax.Shape...]
where the time goes in v4:
time: 133 us
  Pallas kernels  130 us (98%)
  local copies, waits for them, and re-layouts  2.34 us (2%)
    pallas_call x1, Pallas kernels, on_device(): pl.pallas_call(functools.partial(moe_kernel, n_exp), out_shape=(jax.Shape...  130 us

profile of v4, /device:TPU:1, one launch (start us, length us, event | category | flops | bytes accessed | tf_op | source)
XLA Modules:
  0.0 132.8 jit_solution(1257223235791788759)
XLA Ops:
  0.6 129.8 %shard_map.95 = (bf16[1,8,5120]{2,1,0:T(8,128)(2,1)}, bf16[128,1024]{1,0:T(8,128)(2,1)}) custom-call(bf16[1,8,5120]{2,1,0:T(8,128)(2,1)} %tok_ref.1, s32[6,1,8]{2,1,0:T(1,128)} %bitcast.4, f32[6,1,8]{2,1,0:T(1,128)} %bitcast.5, bf16[128,1152]{1,0:T(8,128)(2,1)} %q_ref.1, bf16[576,128]{1,0:T(8,128)(2,1)} %bitcast.3, bf16[1,96,5120]{2,1,0:T(8,128)(2,1)} %wg_ref.1, ...), custom_call_target="tpu_custom_call" | custom-call | tf_op jit(solution)/shard_map/pallas_call | solution.py:347
  130.4 0.0 copy-start
  130.4 1.7 %copy.12 = bf16[128,1024]{1,0:T(8,128)(2,1)} copy(bf16[128,1024]{1,0:T(8,128)(2,1)} %get-tuple-element.8) | data formatting | bytes 524288
  132.1 0.0 copy-done
  132.1 0.6 copy.13
Async XLA Ops:
  130.4 1.7 %copy-start = (bf16[1,8,5120]{2,1,0:T(8,128)(2,1)S(1)}, bf16[1,8,5120]{2,1,0:T(8,128)(2,1)}, u32[]{:S(2)}) copy-start(bf16[1,8,5120]{2,1,0:T(8,128)(2,1)} %get-tuple-element.9) | copy-start | bytes 245764

commit v5 on v4

--- a/solution.py
+++ b/solution.py
@@ -330,6 +330,21 @@
     remote(wide_send.at[others], wide_send.at[others], wide_s, wide_r, me).wait_send()
     for k in range(NX):
         remote(y_send.at[k, others], y_send.at[k, others], y_s.at[k], y_r.at[k], me).wait_send()
+
+
+def settle_kernel(a_ref, b_ref, a_out, b_out):
+    a_out[...] = a_ref[...]
+    b_out[...] = b_ref[...]
+
+
+def settle(a, b):
+    whole = pl.BlockSpec(memory_space=pltpu.VMEM)
+    return pl.pallas_call(
+        settle_kernel,
+        out_shape=(jax.ShapeDtypeStruct(a.shape, a.dtype), jax.ShapeDtypeStruct(b.shape, b.dtype)),
+        in_specs=[whole, whole],
+        out_specs=(whole, whole),
+    )(a, b)
 
 
 def on_device(hidden, queries, latents, expert_ids, route_weight, w_gate, w_up, w_down):
@@ -384,7 +399,7 @@
             collective_id=0, has_side_effects=True, vmem_limit_bytes=56 << 20
         ),
     )(hidden, jnp.transpose(expert_ids, (2, 0, 1)), jnp.transpose(route_weight, (2, 0, 1)), queries, latents.T, w_gate, w_up, w_down)
-    return attended, moe_out
+    return settle(attended, moe_out)
 
 
 def solution(mesh):

time: 133 us -> 132 us (level)
  local copies, waits for them, and re-layouts: 2.34 us -> 0 us
    unnamed x4 -> x0, local copies, waits for them, and re-layouts: 2.34 us -> none
    pallas_call x0 -> x1, Pallas kernels: none -> 1.71 us  [settle(): pl.pallas_call(settle_kernel, out_shape=(jax.ShapeDtypeStruct(a.shape, a....]
where the time goes in v5:
time: 132 us
  Pallas kernels  131 us (99%)
    pallas_call x1, Pallas kernels, on_device(): pl.pallas_call(functools.partial(moe_kernel, n_exp), out_shape=(jax.Shape...  130 us

profile of v5, /device:TPU:1, one launch (start us, length us, event | category | flops | bytes accessed | tf_op | source)
XLA Modules:
  0.0 132.1 jit_solution(18164625392226868865)
XLA Ops:
  0.6 129.8 %shard_map.95 = (bf16[1,8,5120]{2,1,0:T(8,128)(2,1)}, bf16[128,1024]{1,0:T(8,128)(2,1)}) custom-call(bf16[1,8,5120]{2,1,0:T(8,128)(2,1)} %tok_ref.1, s32[6,1,8]{2,1,0:T(1,128)} %bitcast.4, f32[6,1,8]{2,1,0:T(1,128)} %bitcast.5, bf16[128,1152]{1,0:T(8,128)(2,1)} %q_ref.1, bf16[576,128]{1,0:T(8,128)(2,1)} %bitcast.3, bf16[1,96,5120]{2,1,0:T(8,128)(2,1)} %wg_ref.1, ...), custom_call_target="tpu_custom_call" | custom-call | tf_op jit(solution)/shard_map/pallas_call | solution.py:362
  130.4 1.7 %shard_map.96 = (bf16[128,1024]{1,0:T(8,128)(2,1)}, bf16[1,8,5120]{2,1,0:T(8,128)(2,1)}) custom-call(bf16[128,1024]{1,0:T(8,128)(2,1)} %get-tuple-element.4.a_ref, bf16[1,8,5120]{2,1,0:T(8,128)(2,1)} %get-tuple-element.5.b_ref), custom_call_target="tpu_custom_call" | custom-call | tf_op jit(solution)/shard_map/pallas_call | solution.py:342
